TPU v7x, 512 devices: a whole 4x8x8 slice. The times are simulated.
512 devices in a mesh: tm: 64 (over z, x, core), band: 8 (over y).
Axes of the slice: x: 4, y: 8, z: 8, core: 2. Of those that a mesh axis runs over, the one named last changes fastest.
Arguments:
- query_input: bfloat16 [64, 40, 26, 1120], P('tm', 'band'), may hold values from -6 to 6
- key_input: bfloat16 [64, 40, 26, 1120], P('tm', 'band'), may hold values from -8 to 8
- value_input: bfloat16 [64, 40, 26, 1120], P('tm', 'band'), may hold values from -12 to 12
- cotangent: bfloat16 [64, 40, 26, 1120], P('tm', 'band'), may hold values from -6 to 6
- local_kernel_weight: float32 [3, 3, 1120], replicated, may hold values from -2 to 2
Outputs:
- mixed_out: bfloat16 [64, 40, 26, 1120], P('tm', 'band')
- query_grad: bfloat16 [64, 40, 26, 1120], P('tm', 'band')
- key_grad: bfloat16 [64, 40, 26, 1120], P('tm', 'band')
- value_grad: bfloat16 [64, 40, 26, 1120], P('tm', 'band')
- kernel_grad: float32 [3, 3, 1120], replicated
All inputs are finite; a program needn't handle non-finite values.
Results may differ from a plain program's by a relative error of at most 0.018.
Values may be sent and summed in bfloat16 or wider, within the bound.
No kernel may reach another device: no remote copies, remote signals or barrier semaphores. Data moves between devices by JAX's collectives and lax.ppermute only.
A program may use at most 128 MiB of HBM per device.

v0:
```python
import math
import jax
import jax.numpy as jnp
from jax import lax
from jax.sharding import PartitionSpec as P

HEADS = 35
HEAD_DIM = 32


def entering(shard, axis, combine, identity, reverse):
    devices, mine = (lax.axis_size(axis), lax.axis_index(axis))
    everything = jax.tree.map(lambda part: lax.all_gather(part, axis), shard)
    start = jax.tree.map(
        lambda part, zero: jnp.broadcast_to(jnp.asarray(zero, part.dtype), part.shape),
        shard,
        identity,
    )

    def step(k, before):
        at = devices - 1 - k if reverse else k
        reached = at > mine if reverse else at < mine
        new = combine(before, jax.tree.map(lambda part: part[at], everything))
        return jax.tree.map(lambda a, b: jnp.where(reached, a, b), new, before)

    return lax.fori_loop(0, devices, step, start)


def padded(cells, sides, width):
    for axis, dim in sides:
        count = lax.axis_size(axis)
        ends = count - 1
        head = lax.slice_in_dim(cells, 0, width, axis=dim)
        tail = lax.slice_in_dim(cells, cells.shape[dim] - width, cells.shape[dim], axis=dim)
        cells = jnp.concatenate(
            [
                lax.ppermute(tail, axis, [(i, (i + 1) % count) for i in range(ends)]),
                cells,
                lax.ppermute(head, axis, [((i + 1) % count, i) for i in range(ends)]),
            ],
            axis=dim,
        )
    return cells


def feature(x):
    return jnp.where(x > 0, x + 1.0, jnp.exp(jnp.minimum(x, 0.0)))


def slope(x):
    return jnp.where(x > 0, jnp.ones_like(x), jnp.exp(jnp.minimum(x, 0.0)))


def add_pair(earlier, later_term):
    return (earlier[0] + later_term[0], earlier[1] + later_term[1])


def frame_totals(terms, backward):
    frame = lax.psum(terms, "band")
    start = (jnp.zeros_like(frame[0]), jnp.zeros_like(frame[1]))
    before = entering(frame, "tm", add_pair, start, backward)
    return add_pair(before, frame)


def group_heads_count():
    chosen = 1
    for candidate in range(1, HEADS + 1):
        if HEADS % candidate == 0 and candidate * HEAD_DIM <= 256:
            chosen = candidate
    return chosen


def block_outer(left, right, group_count, group_heads, precise):
    count = left.shape[0]
    group_width = group_heads * HEAD_DIM
    left_groups = left.reshape(count, group_count, group_width)
    right_groups = right.reshape(count, group_count, group_width)
    if precise:
        whole = jnp.einsum(
            "tga,tgb->gab", left_groups, right_groups, precision=lax.Precision.HIGHEST
        )
    else:
        whole = jnp.einsum(
            "tga,tgb->gab", left_groups, right_groups, preferred_element_type=jnp.float32
        )
    whole = whole.reshape(group_count, group_heads, HEAD_DIM, group_heads, HEAD_DIM)
    same_head = jnp.eye(group_heads, dtype=jnp.float32)[None, :, None, :, None]
    return jnp.sum(whole * same_head, axis=3).reshape(HEADS, HEAD_DIM, HEAD_DIM)


def block_matrix(state, group_count, group_heads):
    group_width = group_heads * HEAD_DIM
    placed = state.reshape(group_count, group_heads, HEAD_DIM, 1, HEAD_DIM)
    same_head = jnp.eye(group_heads, dtype=jnp.float32)[None, :, None, :, None]
    return (placed * same_head).reshape(group_count, group_width, group_width)


def apply_blocks(rows, blocks, transposed):
    count = rows.shape[0]
    group_count, group_width = (blocks.shape[0], blocks.shape[1])
    grouped = rows.reshape(count, group_count, group_width)
    if transposed:
        result = jnp.einsum("tgb,gab->tga", grouped, blocks, precision=lax.Precision.HIGHEST)
    else:
        result = jnp.einsum("tga,gab->tgb", grouped, blocks, precision=lax.Precision.HIGHEST)
    return result.reshape(count, group_count * group_width)


def shards(query_input, key_input, value_input, cotangent, local_kernel_weight):
    high = lax.Precision.HIGHEST
    band_row_span, column_count, width = (
        query_input.shape[1],
        query_input.shape[2],
        query_input.shape[3],
    )
    count = band_row_span * column_count
    group_heads = group_heads_count()
    group_count = HEADS // group_heads
    indicator = (jnp.arange(width)[:, None] // HEAD_DIM == jnp.arange(HEADS)[None, :]).astype(
        jnp.float32
    )
    q_raw = query_input[0].reshape(count, width).astype(jnp.float32)
    k_raw = key_input[0].reshape(count, width).astype(jnp.float32)
    q_feat = feature(q_raw).astype(jnp.bfloat16)
    k_feat = feature(k_raw).astype(jnp.bfloat16)
    value_flat = value_input[0].reshape(count, width)
    own_state = block_outer(k_feat, value_flat, group_count, group_heads, False)
    own_norm = jnp.sum(k_feat, axis=0, dtype=jnp.float32).reshape(HEADS, HEAD_DIM)
    state, norm_vec = frame_totals((own_state, own_norm), False)
    q_wide = q_feat.astype(jnp.float32)
    state_blocks = block_matrix(state, group_count, group_heads)
    norm_flat = norm_vec.reshape(width)
    num = apply_blocks(q_wide, state_blocks, False)
    den = jnp.dot(q_wide * norm_flat, indicator, precision=high)
    den_wide = jnp.dot(den, indicator.T, precision=high)
    attn = num / den_wide
    stacked = jnp.stack([value_input[0], cotangent[0]])
    rimmed = padded(stacked, (("band", 1),), 1)
    padded_input = jnp.pad(rimmed, ((0, 0), (0, 0), (1, 1), (0, 0)))
    value_padded = padded_input[0]
    gpad = padded_input[1]
    complete_gradient = cotangent[0].astype(jnp.float32)
    local_output = jnp.zeros((band_row_span, column_count, width), jnp.float32)
    v_local = jnp.zeros((band_row_span, column_count, width), jnp.float32)
    kernel_row_slice = []
    for row_offset in range(3):
        for column_offset in range(3):
            local_output = (
                local_output
                + local_kernel_weight[row_offset, column_offset]
                * value_padded[
                    row_offset : row_offset + band_row_span,
                    column_offset : column_offset + column_count,
                ]
            )
            v_local = (
                v_local
                + local_kernel_weight[row_offset, column_offset]
                * gpad[
                    2 - row_offset : 2 - row_offset + band_row_span,
                    2 - column_offset : 2 - column_offset + column_count,
                ]
            )
            kernel_row_slice.append(
                jnp.sum(
                    complete_gradient
                    * value_padded[
                        row_offset : row_offset + band_row_span,
                        column_offset : column_offset + column_count,
                    ],
                    axis=(0, 1),
                )
            )
    mixed_out = (attn.reshape(band_row_span, column_count, width) + local_output).astype(
        jnp.bfloat16
    )[None]
    grad_flat = complete_gradient.reshape(count, width)
    scaled = grad_flat / den_wide
    den_grad = -jnp.dot(grad_flat * attn, indicator, precision=high) / den
    den_grad_wide = jnp.dot(den_grad, indicator.T, precision=high)
    back_state = block_outer(q_wide, scaled, group_count, group_heads, True)
    back_norm = jnp.sum(q_wide * den_grad_wide, axis=0).reshape(HEADS, HEAD_DIM)
    later_state, later_norm = frame_totals((back_state, back_norm), True)
    query_grad = apply_blocks(scaled, state_blocks, True) + den_grad_wide * norm_flat
    query_grad = (
        (query_grad * slope(q_raw))
        .reshape(band_row_span, column_count, width)
        .astype(jnp.bfloat16)[None]
    )
    later_blocks = block_matrix(later_state, group_count, group_heads)
    key_grad = apply_blocks(
        value_flat.astype(jnp.float32), later_blocks, True
    ) + later_norm.reshape(width)
    key_grad = (
        (key_grad * slope(k_raw))
        .reshape(band_row_span, column_count, width)
        .astype(jnp.bfloat16)[None]
    )
    value_grad = apply_blocks(k_feat.astype(jnp.float32), later_blocks, False)
    value_grad = (value_grad.reshape(band_row_span, column_count, width) + v_local).astype(
        jnp.bfloat16
    )[None]
    kernel_terms = jnp.stack(kernel_row_slice).reshape(3, 3, width)
    kernel_total = lax.psum(kernel_terms, ("tm", "band"))
    total_tokens = lax.axis_size("tm") * lax.axis_size("band") * count
    kernel_grad = kernel_total / math.sqrt(total_tokens)
    return (mixed_out, query_grad, key_grad, value_grad, kernel_grad)


def solution(mesh):
    placed = (
        P("tm", "band", None, None),
        P("tm", "band", None, None),
        P("tm", "band", None, None),
        P("tm", "band", None, None),
        P(),
    )
    return jax.shard_map(
        shards,
        mesh=mesh,
        in_specs=placed,
        out_specs=(
            P("tm", "band", None, None),
            P("tm", "band", None, None),
            P("tm", "band", None, None),
            P("tm", "band", None, None),
            P(),
        ),
        check_vma=False,
    )
```

profile of v0, /device:TPU:1, one launch (start us, length us, event | category | flops | bytes accessed | tf_op | source)
XLA Modules:
  0.0 863.7 jit_solution(13523367854085724787)
XLA Ops:
  10.0 2.6 reshape.180
  12.5 4.8 multiply_reduce_fusion.1
  17.4 79.9 %all-reduce.4.cloned.1.call-done = f32[35,32,32]{2,1,0:T(8,128)} async-done(((f32[35,32,32]{2,1,0:T(8,128)}), f32[35,32,32]{2,1,0:T(8,128)}) %all-reduce.4.cloned.1.call-update) | async-done | bytes 143376 | tf_op jit(solution)/shard_map/psum | solution.py:59
  97.5 22.3 %psum.36 = f32[35,32]{1,0:T(8,128)S(1)} all-reduce(f32[35,32]{1,0:T(8,128)S(1)} %reshape.182), channel_id=1, replica_groups=mesh['tm'=64,'band'=8] {'band'}, use_global_device_ids=true, to_apply=%region_3.4 | all-reduce | flops 1120 | bytes 8960 | tf_op jit(solution)/shard_map/psum | solution.py:59
  121.4 1.3 select_n.138
  123.8 69.4 %all-gather.4 = f32[64,35,32]{1,2,0:T(8,128)} all-gather(f32[1,35,32]{1,2,0:T(8,128)S(1)} %copy.44), channel_id=3, replica_groups=mesh['tm'=64,'band'=8] {'tm'}, dimensions={0}, use_global_device_ids=true | all-gather | bytes 291200 | tf_op jit(solution)/shard_map/all_gather | solution.py:13
  193.2 69.6 %all-gather.9.cloned.1.call-done = f32[2240,32,32]{2,1,0:T(8,128)} async-done(((f32[35,32,32]{2,1,0:T(8,128)}), f32[2240,32,32]{2,1,0:T(8,128)}) %all-gather.9.cloned.1.call-update) | async-done | bytes 9175056 | tf_op jit(solution)/shard_map/all_gather | solution.py:13
  262.8 135.1 %while.34 = (s32[]{:T(128)}, f32[35,32,32]{2,1,0:T(8,128)S(1)}, f32[35,32]{1,0:T(8,128)S(1)}, s32[]{:T(128)}, f32[64,35,32,32]{3,2,1,0:T(8,128)}, /*index=5*/f32[64,35,32]{1,2,0:T(8,128)}, s32[]{:T(128)}, s32[]{:T(128)}) while((s32[]{:T(128)}, f32[35,32,32]{2,1,0:T(8,128)S(1)}, f32[35,32]{1,0:T(8,128)S(1)}, s32[]{:T(128)}, ...), condition=%wide.region_5.6_spmd.clone, body=%wide.region_4.5_spmd.clone.sunk | while | flops 110884 | bytes 461555 | solution.py:26
  262.8 1.3 add_select_fusion.9
  264.9 1.3 add_select_fusion.9
  267.1 1.3 add_select_fusion.9
  269.2 1.3 add_select_fusion.9
  271.3 1.3 add_select_fusion.9
  273.4 1.3 add_select_fusion.9
  275.5 1.3 add_select_fusion.9
  277.6 1.3 add_select_fusion.9
  279.7 1.3 add_select_fusion.9
  281.8 1.3 add_select_fusion.9
  283.9 1.3 add_select_fusion.9
  286.0 1.3 add_select_fusion.9
  288.1 1.3 add_select_fusion.9
  398.0 2.4 mul.264
  400.4 3.6 mul.265
  405.9 2.4 reshape.183
  409.2 3.0 fusion.73
  412.2 1.5 reshape.185
  413.7 2.0 fusion.49
  415.7 3.9 reshape.187
  419.6 4.8 multiply_reduce_fusion
  424.4 70.0 %all-reduce.6.cloned.1.call-done = f32[35,32,32]{2,1,0:T(8,128)} async-done(((f32[35,32,32]{2,1,0:T(8,128)}), f32[35,32,32]{2,1,0:T(8,128)}) %all-reduce.6.cloned.1.call-update) | async-done | bytes 143376 | tf_op jit(solution)/shard_map/psum | solution.py:59
  494.6 3.2 collective-permute-start
  497.8 1.5 collective-permute-start.1
  499.3 2.0 select_n.142
  501.4 2.2 collective-permute-done.1
  503.6 1.5 fusion.10
  506.2 107.4 %psum.39 = f32[3,3,1120]{2,1,0:T(4,128)S(1)} all-reduce(f32[3,3,1120]{2,1,0:T(4,128)S(1)} %reshape.191), channel_id=1, replica_groups=mesh['tm'=64,'band'=8] {'tm','band'}, use_global_device_ids=true, to_apply=%region_21.22 | all-reduce | flops 10080 | bytes 80640 | tf_op jit(solution)/shard_map/psum | solution.py:204
  614.3 3.1 convolution_bitcast_fusion.3
  618.8 2.1 reshape.184
  620.9 2.2 fusion.4
  624.0 24.1 %psum.38 = f32[35,32]{1,0:T(8,128)S(1)} all-reduce(f32[35,32]{1,0:T(8,128)S(1)} %reshape.189), channel_id=1, replica_groups=mesh['tm'=64,'band'=8] {'band'}, use_global_device_ids=true, to_apply=%region_9.10 | all-reduce | flops 1120 | bytes 8960 | tf_op jit(solution)/shard_map/psum | solution.py:59
  649.0 58.1 %all-gather.5 = f32[64,35,32]{1,2,0:T(8,128)} all-gather(f32[1,35,32]{1,2,0:T(8,128)S(1)} %copy.52), channel_id=5, replica_groups=mesh['tm'=64,'band'=8] {'tm'}, dimensions={0}, use_global_device_ids=true | all-gather | bytes 291200 | tf_op jit(solution)/shard_map/all_gather | solution.py:13
  707.0 1.4 fusion.52
  708.4 135.5 %while.35 = (s32[]{:T(128)}, f32[35,32,32]{2,1,0:T(8,128)S(1)}, f32[35,32]{1,0:T(8,128)S(1)}, s32[]{:T(128)}, f32[64,35,32,32]{3,2,1,0:T(8,128)}, /*index=5*/f32...) while((s32[]{:T(128)}, f32[35,32,32]{2,1,0:T(8,128)S(1)}, ...), condition=%wide.region_11.12_spmd.clone, body=%wide.region_10.11_spmd.clone.sunk | while | flops 110888 | bytes 461617 | solution.py:26
  708.4 1.3 add_select_fusion.11
  844.0 2.4 mul.306
  846.4 3.6 mul.307
  851.1 1.8 convolution_bitcast_fusion.1
  854.8 1.4 fusion.53
  (608 shorter events, 267.0 us)
Async XLA Ops:
  7.2 1.8 copy-start.17
  7.2 90.1 %all-reduce.4.cloned.1.call-start = ((), (), s32[]{:S(2)}) async-start(), calls=%async_computation | async-start | bytes 1146880 | tf_op jit(solution)/shard_map/psum | solution.py:59
  9.0 1.0 copy-start.5
  9.5 3.0 copy-start.7
  17.4 245.4 %all-gather.9.cloned.1.call-start = ((), (), s32[]{:S(2)}) async-start(), calls=%async_computation.2 | async-start | bytes 37273600 | tf_op jit(solution)/shard_map/all_gather | solution.py:13
  97.3 22.9 %copy-start.20 = (bf16[1,5,26,1120]{3,2,1,0:T(8,128)(2,1)S(1)}, bf16[1,5,26,1120]{3,2,1,0:T(8,128)(2,1)}, u32[]{:S(2)}) copy-start(bf16[1,5,26,1120]{3,2,1,0:T(8,128)(2,1)} %param.9) | copy-start | bytes 873604
  97.3 397.1 %all-reduce.6.cloned.1.call-start = ((), (), s32[]{:S(2)}) async-start(), calls=%async_computation.1 | async-start | bytes 1146880 | tf_op jit(solution)/shard_map/psum | solution.py:59
  121.4 1.4 copy-start.3
  122.7 285.6 %copy-start.1 = (f32[130,1120]{1,0:T(8,128)}, f32[130,1120]{1,0:T(8,128)S(1)}, u32[]{:S(2)}) copy-start(f32[130,1120]{1,0:T(8,128)S(1)} %reshape.192) | copy-start | bytes 1747204
  262.8 135.1 %copy-start.16 = (f32[35,32,32]{2,1,0:T(8,128)S(1)}, f32[35,32,32]{2,1,0:T(8,128)}, u32[]{:S(2)}) copy-start(f32[35,32,32]{2,1,0:T(8,128)} %all-reduce.4.cloned.1.call-done) | copy-start | bytes 430084
  400.4 3.6 copy-start.9
  412.2 1.5 copy-start.10
  413.7 5.8 copy-start
  424.4 70.1 %copy-start.18 = (bf16[1,5,26,1120]{3,2,1,0:T(8,128)(2,1)S(1)}, bf16[1,5,26,1120]{3,2,1,0:T(8,128)(2,1)}, u32[]{:S(2)}) copy-start(bf16[1,5,26,1120]{3,2,1,0:T(8,128)(2,1)} %param.11) | copy-start | bytes 873604
  424.4 284.0 %all-gather.11.cloned.1.call-start = ((), (), s32[]{:S(2)}) async-start(), calls=%async_computation.3 | async-start | bytes 37273600 | tf_op jit(solution)/shard_map/all_gather | solution.py:13
  494.5 3.2 copy-start.12
  494.5 6.8 copy-start.21
  494.6 6.9 collective-permute-start
  497.8 5.9 collective-permute-start.1
  618.8 4.3 copy-start.2
  620.9 2.2 copy-start.13
  620.9 2.2 copy-start.14
  623.9 83.1 %copy-start.4 = (f32[5,26,1120]{2,1,0:T(8,128)S(1)}, f32[5,26,1120]{2,1,0:T(8,128)}, u32[]{:S(2)}) copy-start(f32[5,26,1120]{2,1,0:T(8,128)} %reshape.184) | copy-start | bytes 1747204
  708.4 135.5 %copy-start.15 = (f32[35,32,32]{2,1,0:T(8,128)S(1)}, f32[35,32,32]{2,1,0:T(8,128)}, u32[]{:S(2)}) copy-start(f32[35,32,32]{2,1,0:T(8,128)} %all-reduce.6.cloned.1.call-done) | copy-start | bytes 430084
  846.4 3.6 copy-start.6
  850.0 1.0 copy-start.8
  853.1 1.1 copy-start.11
  854.8 1.4 copy-start.19
Sparse Core Ops, SparseCore 0:
  17.5 79.7 all-reduce.3
  100.6 162.1 all-gather.8
  424.5 69.8 all-reduce.5
  497.6 161.7 all-gather.10
where the time goes:
time: 877 us; the launch traced here: 864 us
  blocking collectives  281 us (32%)
  waiting for transfers between devices  222 us (25%)
  other arithmetic  182 us (21%)
  local copies, waits for them, and re-layouts  141 us (16%)
  matrix products  15.3 us (2%)
  between operations  14.3 us (2%)
    select_n x256, other arithmetic, step(): return jax.tree.map(lambda a, b: jnp.where(reached, a, b), new, before)  163 us
    psum x2, waiting for transfers between devices, frame_totals(): frame = lax.psum(terms, 'band')  150 us
    all_gather x2, blocking collectives, entering(): everything = jax.tree.map(lambda part: lax.all_gather(part, axis), shard)  127 us
    psum x1, blocking collectives, shards(): kernel_total = lax.psum(kernel_terms, ('tm', 'band'))  107 us
    dynamic_slice x256, local copies, waits for them, and re-layouts, step(): new = combine(before, jax.tree.map(lambda part: part[at], everything))  104 us
    all_gather x2, waiting for transfers between devices, entering(): everything = jax.tree.map(lambda part: lax.all_gather(part, axis), shard)  69.6 us
    psum x2, blocking collectives, frame_totals(): frame = lax.psum(terms, 'band')  46.4 us
  transfers between devices with their start and end apart: 6, of which 4 were waited for; matrix products, arithmetic and copies ran while one was open for 2% of the time, Pallas kernels for 0%

commit v1 on v0

--- a/solution.py
+++ b/solution.py
@@ -201,7 +201,7 @@
         jnp.bfloat16
     )[None]
     kernel_terms = jnp.stack(kernel_row_slice).reshape(3, 3, width)
-    kernel_total = lax.psum(kernel_terms, ("tm", "band"))
+    kernel_total = jnp.sum(lax.all_gather(kernel_terms, ("tm", "band")), axis=0)
     total_tokens = lax.axis_size("tm") * lax.axis_size("band") * count
     kernel_grad = kernel_total / math.sqrt(total_tokens)
     return (mixed_out, query_grad, key_grad, value_grad, kernel_grad)

time: 877 us -> 844 us (0.962)
  blocking collectives: 281 us -> 184 us
  waiting for transfers between devices: 222 us -> 276 us
  other arithmetic: 182 us -> 191 us
    psum x1 -> x0, blocking collectives: 107 us -> none  [shards(): kernel_total = lax.psum(kernel_terms, ('tm', 'band'))]
    all_gather x2, waiting for transfers between devices: 69.6 us -> 119 us  [entering(): everything = jax.tree.map(lambda part: lax.all_gather(part, axis), shard)]
    reduce_sum x0 -> x1, other arithmetic: none -> 9.7 us  [shards(): kernel_total = jnp.sum(lax.all_gather(kernel_terms, ('tm', 'band')), axis=0)]
    all_gather x2, blocking collectives: 127 us -> 137 us  [entering(): everything = jax.tree.map(lambda part: lax.all_gather(part, axis), shard)]
  transfers between devices with their start and end apart: 6 -> 7, of which waited for: 4 -> 7; matrix products, arithmetic and copies ran while one was open for 2% -> 20% of each run, Pallas kernels for 0% -> 0%
where the time goes in v1:
time: 844 us; the launch traced here: 830 us
  waiting for transfers between devices  276 us (33%)
  other arithmetic  191 us (23%)
  blocking collectives  184 us (22%)
  local copies, waits for them, and re-layouts  143 us (17%)
  between operations  14.5 us (2%)
  matrix products  14.1 us (2%)
    select_n x256, other arithmetic, step(): return jax.tree.map(lambda a, b: jnp.where(reached, a, b), new, before)  164 us
    psum x2, waiting for transfers between devices, frame_totals(): frame = lax.psum(terms, 'band')  150 us
    all_gather x2, blocking collectives, entering(): everything = jax.tree.map(lambda part: lax.all_gather(part, axis), shard)  137 us
    all_gather x2, waiting for transfers between devices, entering(): everything = jax.tree.map(lambda part: lax.all_gather(part, axis), shard)  119 us
    dynamic_slice x256, local copies, waits for them, and re-layouts, step(): new = combine(before, jax.tree.map(lambda part: part[at], everything))  104 us
    psum x2, blocking collectives, frame_totals(): frame = lax.psum(terms, 'band')  46.8 us
  transfers between devices with their start and end apart: 7, of which 7 were waited for; matrix products, arithmetic and copies ran while one was open for 20% of the time, Pallas kernels for 0%

profile of v1, /device:TPU:1, one launch (start us, length us, event | category | flops | bytes accessed | tf_op | source)
XLA Modules:
  0.0 830.2 jit_solution(11352602187505395984)
XLA Ops:
  10.0 2.6 reshape.177
  12.5 4.8 multiply_reduce_fusion.1
  17.4 79.9 %all-reduce.4.cloned.1.call-done = f32[35,32,32]{2,1,0:T(8,128)} async-done(((f32[35,32,32]{2,1,0:T(8,128)}), f32[35,32,32]{2,1,0:T(8,128)}) %all-reduce.4.cloned.1.call-update) | async-done | bytes 143376 | tf_op jit(solution)/shard_map/psum | solution.py:59
  97.5 22.3 %psum.29 = f32[35,32]{1,0:T(8,128)S(1)} all-reduce(f32[35,32]{1,0:T(8,128)S(1)} %reshape.179), channel_id=1, replica_groups=mesh['tm'=64,'band'=8] {'band'}, use_global_device_ids=true, to_apply=%region_3.4 | all-reduce | flops 1120 | bytes 8960 | tf_op jit(solution)/shard_map/psum | solution.py:59
  121.4 1.3 select_n.138
  123.8 69.3 %all-gather.4 = f32[64,35,32]{1,2,0:T(8,128)} all-gather(f32[1,35,32]{1,2,0:T(8,128)S(1)} %copy.44), channel_id=3, replica_groups=mesh['tm'=64,'band'=8] {'tm'}, dimensions={0}, use_global_device_ids=true | all-gather | bytes 291200 | tf_op jit(solution)/shard_map/all_gather | solution.py:13
  193.2 69.6 %all-gather.12.cloned.1.call-done = f32[2240,32,32]{2,1,0:T(8,128)} async-done(((f32[35,32,32]{2,1,0:T(8,128)}), f32[2240,32,32]{2,1,0:T(8,128)}) %all-gather.12.cloned.1.call-update) | async-done | bytes 9175056 | tf_op jit(solution)/shard_map/all_gather | solution.py:13
  262.8 135.1 %while.34 = (s32[]{:T(128)}, f32[35,32,32]{2,1,0:T(8,128)S(1)}, f32[35,32]{1,0:T(8,128)S(1)}, s32[]{:T(128)}, f32[64,35,32,32]{3,2,1,0:T(8,128)}, /*index=5*/f32[64,35,32]{1,2,0:T(8,128)}, s32[]{:T(128)}, s32[]{:T(128)}) while((s32[]{:T(128)}, f32[35,32,32]{2,1,0:T(8,128)S(1)}, f32[35,32]{1,0:T(8,128)S(1)}, s32[]{:T(128)}, ...), condition=%wide.region_5.6_spmd.clone, body=%wide.region_4.5_spmd.clone.sunk | while | flops 110884 | bytes 461555 | solution.py:26
  262.8 1.3 add_select_fusion.9
  398.0 2.4 mul.264
  400.4 3.6 mul.265
  405.9 2.4 reshape.180
  409.1 3.0 fusion.73
  412.1 1.5 reshape.182
  413.7 2.0 fusion.49
  415.7 3.9 reshape.184
  419.5 4.8 multiply_reduce_fusion
  424.4 70.0 %all-reduce.6.cloned.1.call-done = f32[35,32,32]{2,1,0:T(8,128)} async-done(((f32[35,32,32]{2,1,0:T(8,128)}), f32[35,32,32]{2,1,0:T(8,128)}) %all-reduce.6.cloned.1.call-update) | async-done | bytes 143376 | tf_op jit(solution)/shard_map/psum | solution.py:59
  494.5 3.0 collective-permute-start
  497.6 1.5 collective-permute-start.1
  499.7 3.8 collective-permute-done.1
  505.6 2.0 select_n.142
  507.9 2.8 convolution_bitcast_fusion.3
  512.1 2.1 reshape.181
  514.2 2.2 fusion.4
  517.2 24.5 %psum.31 = f32[35,32]{1,0:T(8,128)S(1)} all-reduce(f32[35,32]{1,0:T(8,128)S(1)} %reshape.186), channel_id=1, replica_groups=mesh['tm'=64,'band'=8] {'band'}, use_global_device_ids=true, to_apply=%region_9.10 | all-reduce | flops 1120 | bytes 8960 | tf_op jit(solution)/shard_map/psum | solution.py:59
  542.6 67.5 %all-gather.5 = f32[64,35,32]{1,2,0:T(8,128)} all-gather(f32[1,35,32]{1,2,0:T(8,128)S(1)} %copy.52), channel_id=5, replica_groups=mesh['tm'=64,'band'=8] {'tm'}, dimensions={0}, use_global_device_ids=true | all-gather | bytes 291200 | tf_op jit(solution)/shard_map/all_gather | solution.py:13
  610.2 1.4 fusion.52
  611.5 48.9 %all-gather.14.cloned.1.call-done = f32[2240,32,32]{2,1,0:T(8,128)} async-done(((f32[35,32,32]{2,1,0:T(8,128)}), f32[2240,32,32]{2,1,0:T(8,128)}) %all-gather.14.cloned.1.call-update) | async-done | bytes 9175056 | tf_op jit(solution)/shard_map/all_gather | solution.py:13
  660.5 136.1 %while.35 = (s32[]{:T(128)}, f32[35,32,32]{2,1,0:T(8,128)S(1)}, f32[35,32]{1,0:T(8,128)S(1)}, s32[]{:T(128)}, f32[64,35,32,32]{3,2,1,0:T(8,128)}, /*index=5*/f32...) while((s32[]{:T(128)}, f32[35,32,32]{2,1,0:T(8,128)S(1)}, ...), condition=%wide.region_11.12_spmd.clone, body=%wide.region_10.11_spmd.clone.sunk | while | flops 110888 | bytes 461617 | solution.py:26
  660.5 1.3 add_select_fusion.11
  730.4 1.3 add_select_fusion.11
  734.7 1.3 add_select_fusion.11
  758.0 1.4 add_select_fusion.11
  764.5 1.3 add_select_fusion.11
  766.7 1.3 add_select_fusion.11
  768.8 1.3 add_select_fusion.11
  775.2 1.3 add_select_fusion.11
  777.4 1.3 add_select_fusion.11
  779.5 1.3 add_select_fusion.11
  781.7 1.3 add_select_fusion.11
  783.8 1.3 add_select_fusion.11
  790.2 1.3 add_select_fusion.11
  796.7 2.4 mul.306
  799.1 3.9 mul.307
  808.7 1.4 fusion.53
  810.1 3.2 all-gather.10.cloned.1.call-done
  813.3 9.7 %reduce_sum.139 = f32[3,3,1120]{2,1,0:T(4,128)S(1)} reduce(f32[512,3,3,1120]{3,2,1,0:T(4,128)} %all-gather.10.cloned.1.call-done, f32[]{:T(128)} %constant.91.clone.1), dimensions={0}, to_apply=%region_21.22 | reduce | flops 5150880 | bytes 20684164 | tf_op jit(solution)/shard_map/reduce_sum | solution.py:204
  (637 shorter events, 270.4 us)
Async XLA Ops:
  7.2 1.8 copy-start.16
  7.2 90.1 %all-reduce.4.cloned.1.call-start = ((), (), s32[]{:S(2)}) async-start(), calls=%async_computation | async-start | bytes 1146880 | tf_op jit(solution)/shard_map/psum | solution.py:59
  9.0 1.0 copy-start.8
  9.5 3.0 copy-start.6
  17.4 245.4 %all-gather.12.cloned.1.call-start = ((), (), s32[]{:S(2)}) async-start(), calls=%async_computation.3 | async-start | bytes 37273600 | tf_op jit(solution)/shard_map/all_gather | solution.py:13
  97.3 22.9 %copy-start.19 = (bf16[1,5,26,1120]{3,2,1,0:T(8,128)(2,1)S(1)}, bf16[1,5,26,1120]{3,2,1,0:T(8,128)(2,1)}, u32[]{:S(2)}) copy-start(bf16[1,5,26,1120]{3,2,1,0:T(8,128)(2,1)} %param.9) | copy-start | bytes 873604
  97.3 397.0 %all-reduce.6.cloned.1.call-start = ((), (), s32[]{:S(2)}) async-start(), calls=%async_computation.1 | async-start | bytes 1146880 | tf_op jit(solution)/shard_map/psum | solution.py:59
  121.4 1.4 copy-start.3
  122.8 285.6 %copy-start.1 = (f32[130,1120]{1,0:T(8,128)}, f32[130,1120]{1,0:T(8,128)S(1)}, u32[]{:S(2)}) copy-start(f32[130,1120]{1,0:T(8,128)S(1)} %reshape.188) | copy-start | bytes 1747204
  262.8 135.1 %copy-start.15 = (f32[35,32,32]{2,1,0:T(8,128)S(1)}, f32[35,32,32]{2,1,0:T(8,128)}, u32[]{:S(2)}) copy-start(f32[35,32,32]{2,1,0:T(8,128)} %all-reduce.4.cloned.1.call-done) | copy-start | bytes 430084
  400.4 3.6 copy-start.10
  412.1 1.5 copy-start.11
  413.7 5.8 copy-start
  424.3 70.1 %copy-start.17 = (bf16[1,5,26,1120]{3,2,1,0:T(8,128)(2,1)S(1)}, bf16[1,5,26,1120]{3,2,1,0:T(8,128)(2,1)}, u32[]{:S(2)}) copy-start(bf16[1,5,26,1120]{3,2,1,0:T(8,128)(2,1)} %param.11) | copy-start | bytes 873604
  424.3 236.1 %all-gather.14.cloned.1.call-start = ((), (), s32[]{:S(2)}) async-start(), calls=%async_computation.4 | async-start | bytes 37273600 | tf_op jit(solution)/shard_map/all_gather | solution.py:13
  494.4 318.9 %all-gather.10.cloned.1.call-start = ((), (), s32[]{:S(2)}) async-start(), calls=%async_computation.2 | async-start | bytes 28366848 | tf_op jit(solution)/shard_map/all_gather | solution.py:204
  494.5 5.1 collective-permute-start
  497.6 5.9 collective-permute-start.1
  504.7 2.9 copy-start.34
  507.8 102.3 %copy-start.20 = (f32[1120]{0:T(1024)}, f32[1120]{0:T(1024)S(1)}, u32[]{:S(2)}) copy-start(f32[1120]{0:T(1024)S(1)} %get-tuple-element.339) | copy-start | bytes 13444
  507.8 102.3 %copy-start.22 = (f32[1120]{0:T(1024)}, f32[1120]{0:T(1024)S(1)}, u32[]{:S(2)}) copy-start(f32[1120]{0:T(1024)S(1)} %get-tuple-element.340) | copy-start | bytes 13444
  507.8 102.3 %copy-start.24 = (f32[1120]{0:T(1024)}, f32[1120]{0:T(1024)S(1)}, u32[]{:S(2)}) copy-start(f32[1120]{0:T(1024)S(1)} %get-tuple-element.341) | copy-start | bytes 13444
  507.8 102.3 %copy-start.26 = (f32[1120]{0:T(1024)}, f32[1120]{0:T(1024)S(1)}, u32[]{:S(2)}) copy-start(f32[1120]{0:T(1024)S(1)} %get-tuple-element.342) | copy-start | bytes 13444
  507.8 102.3 %copy-start.28 = (f32[1120]{0:T(1024)}, f32[1120]{0:T(1024)S(1)}, u32[]{:S(2)}) copy-start(f32[1120]{0:T(1024)S(1)} %get-tuple-element.343) | copy-start | bytes 13444
  507.8 102.3 %copy-start.30 = (f32[1120]{0:T(1024)}, f32[1120]{0:T(1024)S(1)}, u32[]{:S(2)}) copy-start(f32[1120]{0:T(1024)S(1)} %get-tuple-element.344) | copy-start | bytes 13444
  507.8 102.3 %copy-start.32 = (f32[1120]{0:T(1024)}, f32[1120]{0:T(1024)S(1)}, u32[]{:S(2)}) copy-start(f32[1120]{0:T(1024)S(1)} %get-tuple-element.345) | copy-start | bytes 13444
  512.1 4.3 copy-start.2
  514.2 2.2 copy-start.12
  514.2 2.2 copy-start.13
  517.1 93.0 %copy-start.5 = (f32[5,26,1120]{2,1,0:T(8,128)S(1)}, f32[5,26,1120]{2,1,0:T(8,128)}, u32[]{:S(2)}) copy-start(f32[5,26,1120]{2,1,0:T(8,128)} %reshape.181) | copy-start | bytes 1747204
  660.5 136.1 %copy-start.14 = (f32[35,32,32]{2,1,0:T(8,128)S(1)}, f32[35,32,32]{2,1,0:T(8,128)}, u32[]{:S(2)}) copy-start(f32[35,32,32]{2,1,0:T(8,128)} %all-reduce.6.cloned.1.call-done) | copy-start | bytes 430084
  799.1 3.9 copy-start.9
  804.0 1.3 copy-start.7
  806.5 1.0 copy-start.18
  807.5 1.1 copy-start.4
  807.5 1.1 copy-start.21
  807.5 1.1 copy-start.23
  807.5 1.1 copy-start.25
  807.5 1.1 copy-start.27
  807.5 1.2 copy-start.29
  807.5 1.2 copy-start.31
  807.5 1.2 copy-start.33
Sparse Core Ops, SparseCore 0:
  17.5 79.7 all-reduce.3
  100.6 162.1 all-gather.11
  424.5 69.8 all-reduce.5
  497.5 162.8 all-gather.13
  665.4 147.8 all-gather.9
